TPU v7x, 128 devices: a whole 4x4x4 slice. The times are simulated.
128 devices in a mesh: gx: 16 (over x, y), gy: 8 (over z, core).
Axes of the slice: x: 4, y: 4, z: 4, core: 2. Of those that a mesh axis runs over, the one named last changes fastest.
Arguments:
- field: float32 [256, 256, 1536], P('gx', 'gy'), may hold values from -24 to 24
- kappa: float32 [256, 256, 1536], P('gx', 'gy'), may hold values from 0.02 to 0.16
- history: float32 [126, 128, 64, 128], P(None, 'gx', 'gy'), may hold values from -2400 to 2400
Outputs:
- field_next: float32 [256, 256, 1536], P('gx', 'gy')
- basis: float32 [128, 128, 64, 128], P(None, 'gx', 'gy')
- factor: float32 [128, 128], replicated
All inputs are finite; a program needn't handle non-finite values.
Results may differ from a plain program's by a relative error of at most 0.00018.
Values sent between devices are 32-bit elements; how exact they have to be, the bound alone decides.
No kernel may reach another device: no remote copies, remote signals or barrier semaphores. Data moves between devices by JAX's collectives and lax.ppermute only.
A program may use at most 192 MiB of HBM per device.

v0:
```python
import jax
import jax.numpy as jnp
from jax import lax
from jax.sharding import PartitionSpec as P


def extended(block, sides, width):
    for axis, dim in sides:
        count = lax.axis_size(axis)
        forward = [(i, i + 1) for i in range(count - 1)]
        backward = [(target, source) for source, target in forward]
        low = lax.ppermute(
            lax.slice_in_dim(block, block.shape[dim] - width, None, axis=dim), axis, forward
        )
        high = lax.ppermute(lax.slice_in_dim(block, 0, width, axis=dim), axis, backward)
        block = jnp.concatenate([low, block, high], axis=dim)
    return block


def advance(field_pad, kappa_pad):
    field_z = jnp.pad(field_pad, ((0, 0), (0, 0), (1, 1)))
    kappa_z = jnp.pad(kappa_pad, ((0, 0), (0, 0), (1, 1)))
    centre = field_z[1:-1, 1:-1, 1:-1]
    kcentre = kappa_z[1:-1, 1:-1, 1:-1]
    places = [
        (slice(2, None), slice(1, -1), slice(1, -1)),
        (slice(None, -2), slice(1, -1), slice(1, -1)),
        (slice(1, -1), slice(2, None), slice(1, -1)),
        (slice(1, -1), slice(None, -2), slice(1, -1)),
        (slice(1, -1), slice(1, -1), slice(2, None)),
        (slice(1, -1), slice(1, -1), slice(None, -2)),
    ]
    change = jnp.zeros_like(centre)
    for place in places:
        change = change + 0.5 * (kcentre + kappa_z[place]) * (field_z[place] - centre)
    return centre + change


def sample(field):
    a, b, c = field.shape
    return field.reshape(a // 2, 2, b // 4, 4, c // 12, 12)[:, 0, :, 0, :, 0]


def body(field, kappa, history):
    both = jnp.stack([field, kappa])
    padded = extended(both, (("gx", 1), ("gy", 2)), 1)
    kappa_pad = padded[1]
    first = advance(padded[0], kappa_pad)
    first_pad = extended(first, (("gx", 0), ("gy", 1)), 1)
    second = advance(first_pad, kappa_pad)
    block = jnp.concatenate([history, sample(first)[None], sample(second)[None]], 0)
    shape = block.shape
    block = block.reshape(shape[0], -1)
    rows_all = block.shape[1] * lax.axis_size("gx") * lax.axis_size("gy")
    gram = jnp.einsum("ar,br->ab", block, block, precision=lax.Precision.HIGHEST) / rows_all
    total = lax.psum(gram, ("gx", "gy"))
    factor = jnp.linalg.cholesky(total).T
    basis = lax.linalg.triangular_solve(factor.T, block, left_side=True, lower=True)
    return (second, basis.reshape(shape), factor)


def solution(mesh):
    placed = (P("gx", "gy", None), P("gx", "gy", None), P(None, "gx", "gy", None))
    return jax.shard_map(
        body,
        mesh=mesh,
        in_specs=placed,
        out_specs=(P("gx", "gy", None), P(None, "gx", "gy", None), P()),
        check_vma=False,
    )
```

profile of v0, /device:TPU:1, one launch (start us, length us, event | category | flops | bytes accessed | tf_op | source)
XLA Modules:
  0.0 410.7 jit_solution(8603581438563554559)
XLA Ops:
  7.2 0.0 all-reduce.5.cloned.1.call-start
  7.2 0.0 copy-start
  7.2 0.0 copy-start.1
  7.2 1.4 pad_maximum_fusion.11
  8.7 4.2 %collective-permute-start = (f32[2,1,32,1536]{3,2,1,0:T(8,128)S(1)}, f32[2,1,32,1536]{3,2,1,0:T(8,128)S(1)}, u32[]{:S(2)}, u32[]{:S(2)}) collective-permute-start(f32[2,1,32,1536]{3,2,1,0:T(8,128)S(1)} %get-tuple-element.19), channel_id=1, source_target_pairs={{0,8},{8,16},{16,24},{24,32},{32,40},{40,48},{48,56},{56,64},{64,7... | collective-permute-start | bytes 1179656 | tf_op jit(solution)/shard_map/ppermute | solution.py:12
  12.8 1.3 collective-permute-start.1
  14.1 6.5 %collective-permute-done = f32[2,1,32,1536]{3,2,1,0:T(8,128)S(1)} collective-permute-done((f32[2,1,32,1536]{3,2,1,0:T(8,128)S(1)}, f32[2,1,32,1536]{3,2,1,0:T(8,128)S(1)}, u32[]{:S(2)}, u32[]{:S(2)}) %collective-permute-start) | collective-permute-done | bytes 393248 | tf_op jit(solution)/shard_map/ppermute | solution.py:12
  20.6 3.9 collective-permute-done.1
  24.4 0.0 copy-done
  24.4 0.0 copy-done.1
  24.5 0.3 pad_maximum_fusion.15
  24.8 5.2 %collective-permute-start.2 = (f32[2,18,1,1536]{3,2,1,0:T(1,128)S(1)}, f32[2,18,1,1536]{3,2,1,0:T(1,128)S(1)}, u32[]{:S(2)}, u32[]{:S(2)}) collective-permute-start(f32[2,18,1,1536]{3,2,1,0:T(1,128)S(1)} %get-tuple-element.17), channel_id=1, source_target_pairs={{0,1},{1,2},{2,3},{3,4},{4,5},{5,6},{6,7},{8,9},{9,10},{10,11},{11... | collective-permute-start | bytes 663560 | tf_op jit(solution)/shard_map/ppermute | solution.py:12
  30.1 1.9 collective-permute-start.3
  32.0 0.9 collective-permute-done.2
  32.9 4.4 %collective-permute-done.3 = f32[2,18,1,1536]{3,2,1,0:T(1,128)S(1)} collective-permute-done((f32[2,18,1,1536]{3,2,1,0:T(1,128)S(1)}, f32[2,18,1,1536]{3,2,1,0:T(1,128)S(1)}, u32[]{:S(2)}, u32[]{:S(2)}) %collective-permute-start.3) | collective-permute-done | bytes 221216 | tf_op jit(solution)/shard_map/ppermute | solution.py:15
  37.3 1.7 pad_maximum_fusion
  39.0 4.2 %slice_bitcast_fusion = (f32[18,34,1536]{2,1,0:T(8,128)}, f32[18,34,1536]{2,1,0:T(8,128)}) fusion(f32[2,18,34,1536]{3,2,1,0:T(8,128)S(1)} %pad_maximum_fusion), kind=kLoop, calls=%fused_computation.12 | loop fusion | bytes 15040512 | tf_op jit(solution)/shard_map/squeeze | solution.py:47
  43.2 28.3 %fusion.15 = f32[16,32,1536]{2,1,0:T(8,128)S(1)} fusion(f32[18,34,1536]{2,1,0:T(8,128)} %get-tuple-element.16, f32[18,34,1536]{2,1,0:T(8,128)} %get-tuple-element.15), kind=kLoop, calls=%fused_computation.29 | loop fusion | flops 23592960 | bytes 43450368 | tf_op jit(solution)/shard_map/add | solution.py:36
  71.5 0.0 copy-start.2
  71.6 1.6 collective-permute-start.4
  73.1 4.0 collective-permute-start.5
  77.1 1.1 collective-permute-done.4
  78.2 1.5 collective-permute-done.5
  79.7 0.2 pad_maximum_fusion.16
  79.9 0.7 copy.42
  80.6 1.9 collective-permute-start.6
  82.5 0.7 copy.44
  83.1 4.0 collective-permute-start.7
  87.2 0.0 copy-done.2
  87.2 4.3 %copy.50 = f32[126,8,8,128]{3,0,2,1:T(8,128)} copy(f32[126,8,8,128]{3,2,1,0:T(8,128)S(1)} %copy-done.2) | data formatting | bytes 8257536 | tf_op args[2]
  91.5 5.9 %copy.63 = f32[126,8,8,128]{0,3,2,1:T(8,128)} copy(f32[126,8,8,128]{3,2,1,0:T(8,128)} %param.5) | data formatting | bytes 8257536 | tf_op jit(solution)/shard_map/concatenate | solution.py:51
  97.5 38.1 %reshape.29 = f32[8,2,8,4,128,12]{5,4,3,2,1,0:T(8,128)} reshape(f32[16,32,1536]{2,1,0:T(8,128)S(1)} %fusion.15) | data formatting | bytes 6291456 | tf_op jit(solution)/shard_map/reshape | solution.py:41
  135.6 4.7 %slice.184 = f32[8,1,8,1,128,1]{5,4,3,2,1,0:T(8,128)} slice(f32[8,2,8,4,128,12]{5,4,3,2,1,0:T(8,128)} %reshape.29), slice={[0:8], [0:1], [0:8], [0:1], [0:128], [0:1]} | slice | bytes 65536 | tf_op jit(solution)/shard_map/slice | solution.py:41
  140.3 3.4 copy.64
  143.8 3.3 copy.54
  147.1 0.0 collective-permute-done.6
  147.1 1.0 copy.43
  148.1 0.0 collective-permute-done.7
  148.1 0.0 slice-start
  148.1 1.2 copy.45
  149.3 0.0 slice-start.1
  149.3 4.7 %select_maximum_fusion = f32[18,34,1538]{2,1,0:T(8,128)S(1)} fusion(f32[18,1,1536]{2,1,0:T(1,128)S(1)} %copy.43, f32[18,1,1536]{2,1,0:T(1,128)S(1)} %copy.45, f32[1,32,1536]{2,1,0:T(8,128)S(1)} %collective-permute-done.4, f32[16,32,1536]{2,1,0:T(8,128)S(1)} %fusion.15, f32[1,32,1536]{2,1,0:T(8,128)S(1)} %collective-permute-done.5), kind=kLoop, calls=%fused_computation.3 | loop fusion | flops 11295072 | bytes 7525152 | tf_op jit(solution)/shard_map/concatenate | solution.py:16
  154.0 0.0 slice-done
  154.0 0.0 slice-done.1
  154.0 12.9 %fusion.20 = f32[16,32,1536]{2,1,0:T(8,128)} fusion(f32[16,32,1536]{2,1,0:T(8,128)S(1)} %fusion.15, f32[18,34,1538]{2,1,0:T(8,128)S(1)} %select_maximum_fusion, f32[18,1,1536]{2,1,0:T(1,128)S(1)} %copy.45, f32[1,32,1536]{2,1,0:T(8,128)S(1)} %collective-permute-done.4, f32[1,32,1536]{2,1,0:T(8,128)S(1)} %collective-permute-done.5, ...), kind=kLoop, calls=%fused_computation.35 | loop fusion | flops 29884416 | bytes 33349632 | tf_op jit(solution)/shard_map/add | solution.py:36
  167.0 39.1 %reshape.30 = f32[8,2,8,4,128,12]{5,4,3,2,1,0:T(8,128)} reshape(f32[16,32,1536]{2,1,0:T(8,128)} %fusion.20) | data formatting | bytes 6291456 | tf_op jit(solution)/shard_map/reshape | solution.py:41
  206.1 4.7 %slice.185 = f32[8,1,8,1,128,1]{5,4,3,2,1,0:T(8,128)} slice(f32[8,2,8,4,128,12]{5,4,3,2,1,0:T(8,128)} %reshape.30), slice={[0:8], [0:1], [0:8], [0:1], [0:128], [0:1]} | slice | bytes 65536 | tf_op jit(solution)/shard_map/slice | solution.py:41
  210.8 0.0 copy-start.3
  210.8 2.8 copy.65
  213.7 0.0 copy-done.3
  213.7 7.7 %fusion.48 = f32[128,128]{0,1:T(8,128)} fusion(f32[1,8,8,128]{3,0,2,1:T(1,128)S(1)} %bitcast.44, f32[1,8,8,128]{3,0,2,1:T(1,128)S(1)} %bitcast.43, f32[126,8,8,128]{3,0,2,1:T(8,128)} %copy.50), kind=kOutput, calls=%fused_computation.78 | convolution fusion | flops 1612726272 | bytes 4259840 | tf_op jit(solution)/shard_map/ar,br->ab/dot_general | solution.py:55
  221.4 0.0 all-reduce.5.cloned.1.call-update
  221.4 2.8 copy.55
  224.2 8.9 %pad_maximum_fusion.1 = f32[128,8192]{0,1:T(8,128)} fusion(f32[1,8192]{0,1:T(8,128)} %copy.55, f32[1,8192]{0,1:T(8,128)} %copy.54, f32[126,8192]{0,1:T(8,128)} %bitcast.40), kind=kLoop, calls=%fused_computation.20 | loop fusion | flops 2097152 | bytes 8388608 | tf_op jit(solution)/shard_map/concatenate | solution.py:51
  233.1 135.0 %all-reduce.5.cloned.1.call-done = f32[128,128]{0,1:T(8,128)} async-done(((f32[128,128]{0,1:T(8,128)}), f32[128,128]{0,1:T(8,128)}) %all-reduce.5.cloned.1.call-update) | async-done | bytes 65552 | tf_op jit(solution)/shard_map/psum | solution.py:56
  368.1 0.9 copy.52
  369.0 0.9 fusion.53
  369.9 11.7 %cholesky.16 = f32[128,128]{1,0:T(8,128)S(1)} custom-call(f32[128,128]{1,0:T(8,128)S(1)} %fusion.53), custom_call_target="Cholesky" | custom-call | tf_op jit(solution)/shard_map/jit(cholesky)/cholesky | solution.py:57
  381.6 0.6 compare_reduce_fusion
  382.3 0.7 fusion.54
  382.9 9.8 %custom-call.6 = f32[1,128,128]{1,2,0:T(8,128)S(1)} custom-call(f32[1,128,128]{2,1,0:T(8,128)S(1)} %get-tuple-element.26), custom_call_target="InvertDiagBlocksLowerTriangular" | custom-call | tf_op jit(solution)/shard_map/triangular_solve | solution.py:58
  392.7 5.7 %fusion.51 = f32[128,8,8,128]{3,0,2,1:T(8,128)S(1)} fusion(f32[8,8,128,128]{3,2,1,0:T(8,128)} %bitcast.41, f32[1,128,128]{1,2,0:T(8,128)S(1)} %custom-call.6), kind=kOutput, calls=%fused_computation.88 | convolution fusion | flops 1610612736 | bytes 8454144 | tf_op jit(solution)/shard_map/triangular_solve | solution.py:58
  398.4 4.4 %copy.57 = f32[128,8,8,128]{3,2,1,0:T(8,128)} copy(f32[128,8,8,128]{3,0,2,1:T(8,128)S(1)} %fusion.51) | data formatting | bytes 8388608
  402.9 0.7 copy.58
  (3 shorter events, 0.1 us)
Async XLA Ops:
  7.2 360.9 %all-reduce.5.cloned.1.call-start = ((), (), s32[]{:S(2)}) async-start(), calls=%async_computation | async-start | bytes 131072 | tf_op jit(solution)/shard_map/psum | solution.py:56
  7.2 17.2 %copy-start = (f32[16,32,1536]{2,1,0:T(8,128)S(1)}, f32[16,32,1536]{2,1,0:T(8,128)}, u32[]{:S(2)}) copy-start(f32[16,32,1536]{2,1,0:T(8,128)} %param.4) | copy-start | bytes 9437188
  7.2 17.2 %copy-start.1 = (f32[16,32,1536]{2,1,0:T(8,128)S(1)}, f32[16,32,1536]{2,1,0:T(8,128)}, u32[]{:S(2)}) copy-start(f32[16,32,1536]{2,1,0:T(8,128)} %param.3) | copy-start | bytes 9437188
  8.7 11.9 %collective-permute-start = (f32[2,1,32,1536]{3,2,1,0:T(8,128)S(1)}, f32[2,1,32,1536]{3,2,1,0:T(8,128)S(1)}, u32[]{:S(2)}, u32[]{:S(2)}) collective-permute-start(f32[2,1,32,1536]{3,2,1,0:T(8,128)S(1)} %get-tuple-element.19), channel_id=1, source_target_pairs={{0,8},{8,16},{16,24},{24,32},{32,40},{40,48},{48,56},{56,64},{64,7... | collective-permute-start | bytes 1179656 | tf_op jit(solution)/shard_map/ppermute | solution.py:12
  12.8 11.6 %collective-permute-start.1 = (f32[2,1,32,1536]{3,2,1,0:T(8,128)S(1)}, f32[2,1,32,1536]{3,2,1,0:T(8,128)S(1)}, u32[]{:S(2)}, u32[]{:S(2)}) collective-permute-start(f32[2,1,32,1536]{3,2,1,0:T(8,128)S(1)} %get-tuple-element.20), channel_id=1, source_target_pairs={{8,0},{16,8},{24,16},{32,24},{40,32},{48,40},{56,48},{64,56},{72,6... | collective-permute-start | bytes 1179656 | tf_op jit(solution)/shard_map/ppermute | solution.py:15
  24.8 8.1 %collective-permute-start.2 = (f32[2,18,1,1536]{3,2,1,0:T(1,128)S(1)}, f32[2,18,1,1536]{3,2,1,0:T(1,128)S(1)}, u32[]{:S(2)}, u32[]{:S(2)}) collective-permute-start(f32[2,18,1,1536]{3,2,1,0:T(1,128)S(1)} %get-tuple-element.17), channel_id=1, source_target_pairs={{0,1},{1,2},{2,3},{3,4},{4,5},{5,6},{6,7},{8,9},{9,10},{10,11},{11... | collective-permute-start | bytes 663560 | tf_op jit(solution)/shard_map/ppermute | solution.py:12
  30.1 7.3 %collective-permute-start.3 = (f32[2,18,1,1536]{3,2,1,0:T(1,128)S(1)}, f32[2,18,1,1536]{3,2,1,0:T(1,128)S(1)}, u32[]{:S(2)}, u32[]{:S(2)}) collective-permute-start(f32[2,18,1,1536]{3,2,1,0:T(1,128)S(1)} %get-tuple-element.18), channel_id=1, source_target_pairs={{1,0},{2,1},{3,2},{4,3},{5,4},{6,5},{7,6},{9,8},{10,9},{11,10},{12... | collective-permute-start | bytes 663560 | tf_op jit(solution)/shard_map/ppermute | solution.py:15
  71.5 15.7 %copy-start.2 = (f32[126,8,8,128]{3,2,1,0:T(8,128)S(1)}, f32[126,8,8,128]{3,2,1,0:T(8,128)}, u32[]{:S(2)}) copy-start(f32[126,8,8,128]{3,2,1,0:T(8,128)} %param.5) | copy-start | bytes 12386308
  71.6 6.7 %collective-permute-start.4 = (f32[1,32,1536]{2,1,0:T(8,128)S(1)}, f32[1,32,1536]{2,1,0:T(8,128)S(1)}, u32[]{:S(2)}, u32[]{:S(2)}) collective-permute-start(f32[1,32,1536]{2,1,0:T(8,128)S(1)} %get-tuple-element.24), channel_id=1, source_target_pairs={{8,0},{16,8},{24,16},{32,24},{40,32},{48,40},{56,48},{64,56},{72,6... | collective-permute-start | bytes 589832 | tf_op jit(solution)/shard_map/ppermute | solution.py:15
  73.1 6.6 %collective-permute-start.5 = (f32[1,32,1536]{2,1,0:T(8,128)S(1)}, f32[1,32,1536]{2,1,0:T(8,128)S(1)}, u32[]{:S(2)}, u32[]{:S(2)}) collective-permute-start(f32[1,32,1536]{2,1,0:T(8,128)S(1)} %get-tuple-element.23), channel_id=1, source_target_pairs={{0,8},{8,16},{16,24},{24,32},{32,40},{40,48},{48,56},{56,64},{64,7... | collective-permute-start | bytes 589832 | tf_op jit(solution)/shard_map/ppermute | solution.py:12
  80.6 66.5 %collective-permute-start.6 = (f32[18,1,1536]{2,0,1:T(8,128)}, f32[18,1,1536]{2,0,1:T(8,128)}, u32[]{:S(2)}, u32[]{:S(2)}) collective-permute-start(f32[18,1,1536]{2,0,1:T(8,128)} %copy.42), channel_id=1, source_target_pairs={{1,0},{2,1},{3,2},{4,3},{5,4},{6,5},{7,6},{9,8},{10,9},{11,10},{12... | collective-permute-start | bytes 331784 | tf_op jit(solution)/shard_map/ppermute | solution.py:15
  83.1 65.0 %collective-permute-start.7 = (f32[18,1,1536]{2,0,1:T(8,128)}, f32[18,1,1536]{2,0,1:T(8,128)}, u32[]{:S(2)}, u32[]{:S(2)}) collective-permute-start(f32[18,1,1536]{2,0,1:T(8,128)} %copy.44), channel_id=1, source_target_pairs={{0,1},{1,2},{2,3},{3,4},{4,5},{5,6},{6,7},{8,9},{9,10},{10,11},{11... | collective-permute-start | bytes 331784 | tf_op jit(solution)/shard_map/ppermute | solution.py:12
  148.1 5.9 %slice-start = ((s8[4423680]{0:T(1024)(128)(4,1)}), s8[4194304]{0:T(1024)(128)(4,1)S(1)}, s32[]{:S(2)}) async-start(s8[4423680]{0:T(1024)(128)(4,1)} %bitcast.32), calls=%async_computation.1 | async-start | bytes 8388608
  149.3 4.7 %slice-start.1 = ((s8[4423680]{0:T(1024)(128)(4,1)}), s8[229376]{0:T(1024)(128)(4,1)S(1)}, s32[]{:S(2)}) async-start(s8[4423680]{0:T(1024)(128)(4,1)} %bitcast.32), calls=%async_computation.2 | async-start | bytes 458752
  210.8 2.8 copy-start.3
Sparse Core Ops, SparseCore 0:
  221.5 146.5 all-reduce.4
where the time goes:
time: 419 us; the launch traced here: 411 us
  waiting for transfers between devices  153 us (37%)
  local copies, waits for them, and re-layouts  123 us (29%)
  other arithmetic  82.1 us (20%)
  starting transfers between devices  24.2 us (6%)
  between operations  14.5 us (3%)
  matrix products  13.4 us (3%)
    psum x1, waiting for transfers between devices, body(): total = lax.psum(gram, ('gx', 'gy'))  135 us
    reshape x2, local copies, waits for them, and re-layouts, sample(): return field.reshape(a // 2, 2, b // 4, 4, c // 12, 12)[:, 0, :, 0, :, 0]  77.3 us
    add x2, other arithmetic, advance(): return centre + change  41.3 us
    ppermute x4, starting transfers between devices, extended(): lax.ppermute(lax.slice_in_dim(block, block.shape[dim] - width, None, axis...  17.4 us
    unnamed x17, local copies, waits for them, and re-layouts  15.8 us
    another operation x3, other arithmetic, body(): factor = jnp.linalg.cholesky(total).T  12.4 us
    concatenate x3, local copies, waits for them, and re-layouts, body(): jnp.concatenate([history, sample(first)[None], sample(second)[None]], 0)  12.1 us
    another operation x1, other arithmetic, body(): lax.linalg.triangular_solve(factor.T, block, left_side=True, lower=True)  9.81 us
  transfers between devices with their start and end apart: 9, of which 7 were waited for; matrix products, arithmetic and copies ran while one was open for 18% of the time, Pallas kernels for 0%

commit v1 on v0

--- a/solution.py
+++ b/solution.py
@@ -53,7 +53,7 @@
     block = block.reshape(shape[0], -1)
     rows_all = block.shape[1] * lax.axis_size("gx") * lax.axis_size("gy")
     gram = jnp.einsum("ar,br->ab", block, block, precision=lax.Precision.HIGHEST) / rows_all
-    total = lax.psum(gram, ("gx", "gy"))
+    total = lax.psum(lax.psum(gram, "gx"), "gy")
     factor = jnp.linalg.cholesky(total).T
     basis = lax.linalg.triangular_solve(factor.T, block, left_side=True, lower=True)
     return (second, basis.reshape(shape), factor)

time: 419 us -> 422 us (level)
  local copies, waits for them, and re-layouts: 123 us -> 133 us
  waiting for transfers between devices: 153 us -> 147 us
    unnamed x17, local copies, waits for them, and re-layouts: 15.8 us -> 26.7 us
    psum x1 -> x2, waiting for transfers between devices: 135 us -> 128 us  [body(): total = lax.psum(lax.psum(gram, 'gx'), 'gy')]
  transfers between devices with their start and end apart: 9 -> 10, of which waited for: 7 -> 8; matrix products, arithmetic and copies ran while one was open for 18% -> 17% of each run, Pallas kernels for 0% -> 0%
where the time goes in v1:
time: 422 us; the launch traced here: 414 us
  waiting for transfers between devices  147 us (35%)
  local copies, waits for them, and re-layouts  133 us (32%)
  other arithmetic  82.1 us (19%)
  starting transfers between devices  24.6 us (6%)
  between operations  14.5 us (3%)
  matrix products  13.4 us (3%)
    psum x2, waiting for transfers between devices, body(): total = lax.psum(lax.psum(gram, 'gx'), 'gy')  128 us
    reshape x2, local copies, waits for them, and re-layouts, sample(): return field.reshape(a // 2, 2, b // 4, 4, c // 12, 12)[:, 0, :, 0, :, 0]  77.3 us
    add x2, other arithmetic, advance(): return centre + change  41.3 us
    unnamed x17, local copies, waits for them, and re-layouts  26.7 us
    ppermute x4, starting transfers between devices, extended(): lax.ppermute(lax.slice_in_dim(block, block.shape[dim] - width, None, axis...  17.8 us
    another operation x3, other arithmetic, body(): factor = jnp.linalg.cholesky(total).T  12.4 us
    concatenate x3, local copies, waits for them, and re-layouts, body(): jnp.concatenate([history, sample(first)[None], sample(second)[None]], 0)  10.8 us
    another operation x1, other arithmetic, body(): lax.linalg.triangular_solve(factor.T, block, left_side=True, lower=True)  9.81 us
  transfers between devices with their start and end apart: 10, of which 8 were waited for; matrix products, arithmetic and copies ran while one was open for 17% of the time, Pallas kernels for 0%

profile of v1, /device:TPU:1, one launch (start us, length us, event | category | flops | bytes accessed | tf_op | source)
XLA Modules:
  0.0 414.0 jit_solution(14224669833766496601)
XLA Ops:
  7.2 0.0 all-reduce.6.cloned.1.call-start
  7.2 0.0 copy-start
  7.2 0.0 copy-start.1
  7.2 1.4 pad_maximum_fusion.11
  8.7 4.2 %collective-permute-start = (f32[2,1,32,1536]{3,2,1,0:T(8,128)S(1)}, f32[2,1,32,1536]{3,2,1,0:T(8,128)S(1)}, u32[]{:S(2)}, u32[]{:S(2)}) collective-permute-start(f32[2,1,32,1536]{3,2,1,0:T(8,128)S(1)} %get-tuple-element.19), channel_id=1, source_target_pairs={{0,8},{8,16},{16,24},{24,32},{32,40},{40,48},{48,56},{56,64},{64,7... | collective-permute-start | bytes 1179656 | tf_op jit(solution)/shard_map/ppermute | solution.py:12
  12.8 1.3 collective-permute-start.1
  14.1 6.5 %collective-permute-done = f32[2,1,32,1536]{3,2,1,0:T(8,128)S(1)} collective-permute-done((f32[2,1,32,1536]{3,2,1,0:T(8,128)S(1)}, f32[2,1,32,1536]{3,2,1,0:T(8,128)S(1)}, u32[]{:S(2)}, u32[]{:S(2)}) %collective-permute-start) | collective-permute-done | bytes 393248 | tf_op jit(solution)/shard_map/ppermute | solution.py:12
  20.6 3.9 collective-permute-done.1
  24.4 0.0 copy-done
  24.4 0.0 copy-done.1
  24.5 0.3 pad_maximum_fusion.15
  24.8 5.2 %collective-permute-start.2 = (f32[2,18,1,1536]{3,2,1,0:T(1,128)S(1)}, f32[2,18,1,1536]{3,2,1,0:T(1,128)S(1)}, u32[]{:S(2)}, u32[]{:S(2)}) collective-permute-start(f32[2,18,1,1536]{3,2,1,0:T(1,128)S(1)} %get-tuple-element.17), channel_id=1, source_target_pairs={{0,1},{1,2},{2,3},{3,4},{4,5},{5,6},{6,7},{8,9},{9,10},{10,11},{11... | collective-permute-start | bytes 663560 | tf_op jit(solution)/shard_map/ppermute | solution.py:12
  30.1 1.9 collective-permute-start.3
  32.0 0.9 collective-permute-done.2
  32.9 4.4 %collective-permute-done.3 = f32[2,18,1,1536]{3,2,1,0:T(1,128)S(1)} collective-permute-done((f32[2,18,1,1536]{3,2,1,0:T(1,128)S(1)}, f32[2,18,1,1536]{3,2,1,0:T(1,128)S(1)}, u32[]{:S(2)}, u32[]{:S(2)}) %collective-permute-start.3) | collective-permute-done | bytes 221216 | tf_op jit(solution)/shard_map/ppermute | solution.py:15
  37.3 1.7 pad_maximum_fusion
  39.0 4.2 %slice_bitcast_fusion = (f32[18,34,1536]{2,1,0:T(8,128)}, f32[18,34,1536]{2,1,0:T(8,128)}) fusion(f32[2,18,34,1536]{3,2,1,0:T(8,128)S(1)} %pad_maximum_fusion), kind=kLoop, calls=%fused_computation.12 | loop fusion | bytes 15040512 | tf_op jit(solution)/shard_map/squeeze | solution.py:47
  43.2 28.3 %fusion.15 = f32[16,32,1536]{2,1,0:T(8,128)S(1)} fusion(f32[18,34,1536]{2,1,0:T(8,128)} %get-tuple-element.16, f32[18,34,1536]{2,1,0:T(8,128)} %get-tuple-element.15), kind=kLoop, calls=%fused_computation.29 | loop fusion | flops 23592960 | bytes 43450368 | tf_op jit(solution)/shard_map/add | solution.py:36
  71.5 0.0 copy-start.2
  71.6 1.6 collective-permute-start.4
  73.1 4.0 collective-permute-start.5
  77.1 1.1 collective-permute-done.4
  78.2 1.5 collective-permute-done.5
  79.7 0.2 pad_maximum_fusion.16
  79.9 0.7 copy.42
  80.6 1.9 collective-permute-start.6
  82.5 0.7 copy.44
  83.1 4.4 %collective-permute-start.7 = (f32[18,1,1536]{2,0,1:T(8,128)}, f32[18,1,1536]{2,0,1:T(8,128)}, u32[]{:S(2)}, u32[]{:S(2)}) collective-permute-start(f32[18,1,1536]{2,0,1:T(8,128)} %copy.44), channel_id=1, source_target_pairs={{0,1},{1,2},{2,3},{3,4},{4,5},{5,6},{6,7},{8,9},{9,10},{10,11},{11... | collective-permute-start | bytes 331784 | tf_op jit(solution)/shard_map/ppermute | solution.py:12
  87.6 4.4 %copy.50 = f32[126,8,8,128]{3,0,2,1:T(8,128)} copy(f32[126,8,8,128]{3,2,1,0:T(8,128)S(1)} %copy-done.2) | data formatting | bytes 8257536 | tf_op args[2]
  92.0 38.1 %reshape.29 = f32[8,2,8,4,128,12]{5,4,3,2,1,0:T(8,128)} reshape(f32[16,32,1536]{2,1,0:T(8,128)S(1)} %fusion.15) | data formatting | bytes 6291456 | tf_op jit(solution)/shard_map/reshape | solution.py:41
  130.1 4.7 %slice.184 = f32[8,1,8,1,128,1]{5,4,3,2,1,0:T(8,128)} slice(f32[8,2,8,4,128,12]{5,4,3,2,1,0:T(8,128)} %reshape.29), slice={[0:8], [0:1], [0:8], [0:1], [0:128], [0:1]} | slice | bytes 65536 | tf_op jit(solution)/shard_map/slice | solution.py:41
  134.8 3.4 copy.64
  138.2 0.0 collective-permute-done.6
  138.3 1.0 copy.43
  139.3 0.0 collective-permute-done.7
  139.3 0.0 slice-start
  139.3 1.2 copy.45
  140.5 0.0 slice-start.1
  140.5 4.7 %select_maximum_fusion = f32[18,34,1538]{2,1,0:T(8,128)S(1)} fusion(f32[18,1,1536]{2,1,0:T(1,128)S(1)} %copy.43, f32[18,1,1536]{2,1,0:T(1,128)S(1)} %copy.45, f32[1,32,1536]{2,1,0:T(8,128)S(1)} %collective-permute-done.4, f32[16,32,1536]{2,1,0:T(8,128)S(1)} %fusion.15, f32[1,32,1536]{2,1,0:T(8,128)S(1)} %collective-permute-done.5), kind=kLoop, calls=%fused_computation.3 | loop fusion | flops 11295072 | bytes 7525152 | tf_op jit(solution)/shard_map/concatenate | solution.py:16
  145.2 0.0 slice-done
  145.2 0.0 slice-done.1
  145.2 12.9 %fusion.20 = f32[16,32,1536]{2,1,0:T(8,128)} fusion(f32[16,32,1536]{2,1,0:T(8,128)S(1)} %fusion.15, f32[18,34,1538]{2,1,0:T(8,128)S(1)} %select_maximum_fusion, f32[18,1,1536]{2,1,0:T(1,128)S(1)} %copy.45, f32[1,32,1536]{2,1,0:T(8,128)S(1)} %collective-permute-done.4, f32[1,32,1536]{2,1,0:T(8,128)S(1)} %collective-permute-done.5, ...), kind=kLoop, calls=%fused_computation.35 | loop fusion | flops 29884416 | bytes 33349632 | tf_op jit(solution)/shard_map/add | solution.py:36
  158.1 39.1 %reshape.30 = f32[8,2,8,4,128,12]{5,4,3,2,1,0:T(8,128)} reshape(f32[16,32,1536]{2,1,0:T(8,128)} %fusion.20) | data formatting | bytes 6291456 | tf_op jit(solution)/shard_map/reshape | solution.py:41
  197.3 4.7 %slice.185 = f32[8,1,8,1,128,1]{5,4,3,2,1,0:T(8,128)} slice(f32[8,2,8,4,128,12]{5,4,3,2,1,0:T(8,128)} %reshape.30), slice={[0:8], [0:1], [0:8], [0:1], [0:128], [0:1]} | slice | bytes 65536 | tf_op jit(solution)/shard_map/slice | solution.py:41
  202.0 13.7 %copy.65 = f32[8,1,8,1,128,1]{4,2,0,5,3,1:T(8,128)S(1)} copy(f32[8,1,8,1,128,1]{5,4,3,2,1,0:T(8,128)} %slice.185) | data formatting | bytes 65536
  215.6 7.7 %fusion.48 = f32[128,128]{0,1:T(8,128)} fusion(f32[1,8,8,128]{3,0,2,1:T(1,128)S(1)} %bitcast.44, f32[1,8,8,128]{3,0,2,1:T(1,128)S(1)} %bitcast.42, f32[126,8,8,128]{3,0,2,1:T(8,128)} %copy.50), kind=kOutput, calls=%fused_computation.78 | convolution fusion | flops 1612726272 | bytes 4259840 | tf_op jit(solution)/shard_map/ar,br->ab/dot_general | solution.py:55
  223.4 0.0 all-reduce.6.cloned.1.call-update
  223.4 0.0 all-reduce.8.cloned.1.call-start
  223.4 5.4 %copy.63 = f32[126,8,8,128]{0,3,2,1:T(8,128)} copy(f32[126,8,8,128]{3,2,1,0:T(8,128)} %param.5) | data formatting | bytes 8257536 | tf_op jit(solution)/shard_map/concatenate | solution.py:51
  228.9 2.7 copy.54
  231.5 2.7 copy.55
  234.2 76.0 %all-reduce.6.cloned.1.call-done = f32[128,128]{0,1:T(8,128)} async-done(((f32[128,128]{0,1:T(8,128)}), f32[128,128]{0,1:T(8,128)}) %all-reduce.6.cloned.1.call-update) | async-done | bytes 65552 | tf_op jit(solution)/shard_map/psum | solution.py:56
  310.2 0.0 all-reduce.8.cloned.1.call-update
  310.3 8.9 %pad_maximum_fusion.1 = f32[128,8192]{0,1:T(8,128)} fusion(f32[1,8192]{0,1:T(8,128)} %copy.55, f32[1,8192]{0,1:T(8,128)} %copy.54, f32[126,8192]{0,1:T(8,128)} %bitcast.41), kind=kLoop, calls=%fused_computation.20 | loop fusion | flops 2097152 | bytes 8388608 | tf_op jit(solution)/shard_map/concatenate | solution.py:51
  319.1 52.3 %all-reduce.8.cloned.1.call-done = f32[128,128]{0,1:T(8,128)} async-done(((f32[128,128]{0,1:T(8,128)}), f32[128,128]{0,1:T(8,128)}) %all-reduce.8.cloned.1.call-update) | async-done | bytes 65552 | tf_op jit(solution)/shard_map/psum | solution.py:56
  371.5 0.9 copy.52
  372.4 0.9 fusion.53
  373.3 11.7 %cholesky.16 = f32[128,128]{1,0:T(8,128)S(1)} custom-call(f32[128,128]{1,0:T(8,128)S(1)} %fusion.53), custom_call_target="Cholesky" | custom-call | tf_op jit(solution)/shard_map/jit(cholesky)/cholesky | solution.py:57
  385.0 0.6 compare_reduce_fusion
  385.6 0.7 fusion.54
  386.3 9.8 %custom-call.6 = f32[1,128,128]{1,2,0:T(8,128)S(1)} custom-call(f32[1,128,128]{2,1,0:T(8,128)S(1)} %get-tuple-element.26), custom_call_target="InvertDiagBlocksLowerTriangular" | custom-call | tf_op jit(solution)/shard_map/triangular_solve | solution.py:58
  396.1 5.7 %fusion.51 = f32[128,8,8,128]{3,0,2,1:T(8,128)S(1)} fusion(f32[8,8,128,128]{3,2,1,0:T(8,128)} %bitcast.40, f32[1,128,128]{1,2,0:T(8,128)S(1)} %custom-call.6), kind=kOutput, calls=%fused_computation.88 | convolution fusion | flops 1610612736 | bytes 8454144 | tf_op jit(solution)/shard_map/triangular_solve | solution.py:58
  401.8 4.4 %copy.57 = f32[128,8,8,128]{3,2,1,0:T(8,128)} copy(f32[128,8,8,128]{3,0,2,1:T(8,128)S(1)} %fusion.51) | data formatting | bytes 8388608
  406.2 0.7 copy.58
  (6 shorter events, 0.1 us)
Async XLA Ops:
  7.2 303.1 %all-reduce.6.cloned.1.call-start = ((), (), s32[]{:S(2)}) async-start(), calls=%async_computation | async-start | bytes 131072 | tf_op jit(solution)/shard_map/psum | solution.py:56
  7.2 17.2 %copy-start = (f32[16,32,1536]{2,1,0:T(8,128)S(1)}, f32[16,32,1536]{2,1,0:T(8,128)}, u32[]{:S(2)}) copy-start(f32[16,32,1536]{2,1,0:T(8,128)} %param.4) | copy-start | bytes 9437188
  7.2 17.2 %copy-start.1 = (f32[16,32,1536]{2,1,0:T(8,128)S(1)}, f32[16,32,1536]{2,1,0:T(8,128)}, u32[]{:S(2)}) copy-start(f32[16,32,1536]{2,1,0:T(8,128)} %param.3) | copy-start | bytes 9437188
  8.7 11.9 %collective-permute-start = (f32[2,1,32,1536]{3,2,1,0:T(8,128)S(1)}, f32[2,1,32,1536]{3,2,1,0:T(8,128)S(1)}, u32[]{:S(2)}, u32[]{:S(2)}) collective-permute-start(f32[2,1,32,1536]{3,2,1,0:T(8,128)S(1)} %get-tuple-element.19), channel_id=1, source_target_pairs={{0,8},{8,16},{16,24},{24,32},{32,40},{40,48},{48,56},{56,64},{64,7... | collective-permute-start | bytes 1179656 | tf_op jit(solution)/shard_map/ppermute | solution.py:12
  12.8 11.6 %collective-permute-start.1 = (f32[2,1,32,1536]{3,2,1,0:T(8,128)S(1)}, f32[2,1,32,1536]{3,2,1,0:T(8,128)S(1)}, u32[]{:S(2)}, u32[]{:S(2)}) collective-permute-start(f32[2,1,32,1536]{3,2,1,0:T(8,128)S(1)} %get-tuple-element.20), channel_id=1, source_target_pairs={{8,0},{16,8},{24,16},{32,24},{40,32},{48,40},{56,48},{64,56},{72,6... | collective-permute-start | bytes 1179656 | tf_op jit(solution)/shard_map/ppermute | solution.py:15
  24.8 8.1 %collective-permute-start.2 = (f32[2,18,1,1536]{3,2,1,0:T(1,128)S(1)}, f32[2,18,1,1536]{3,2,1,0:T(1,128)S(1)}, u32[]{:S(2)}, u32[]{:S(2)}) collective-permute-start(f32[2,18,1,1536]{3,2,1,0:T(1,128)S(1)} %get-tuple-element.17), channel_id=1, source_target_pairs={{0,1},{1,2},{2,3},{3,4},{4,5},{5,6},{6,7},{8,9},{9,10},{10,11},{11... | collective-permute-start | bytes 663560 | tf_op jit(solution)/shard_map/ppermute | solution.py:12
  30.1 7.3 %collective-permute-start.3 = (f32[2,18,1,1536]{3,2,1,0:T(1,128)S(1)}, f32[2,18,1,1536]{3,2,1,0:T(1,128)S(1)}, u32[]{:S(2)}, u32[]{:S(2)}) collective-permute-start(f32[2,18,1,1536]{3,2,1,0:T(1,128)S(1)} %get-tuple-element.18), channel_id=1, source_target_pairs={{1,0},{2,1},{3,2},{4,3},{5,4},{6,5},{7,6},{9,8},{10,9},{11,10},{12... | collective-permute-start | bytes 663560 | tf_op jit(solution)/shard_map/ppermute | solution.py:15
  71.5 16.0 %copy-start.2 = (f32[126,8,8,128]{3,2,1,0:T(8,128)S(1)}, f32[126,8,8,128]{3,2,1,0:T(8,128)}, u32[]{:S(2)}) copy-start(f32[126,8,8,128]{3,2,1,0:T(8,128)} %param.5) | copy-start | bytes 12386308
  71.6 6.7 %collective-permute-start.4 = (f32[1,32,1536]{2,1,0:T(8,128)S(1)}, f32[1,32,1536]{2,1,0:T(8,128)S(1)}, u32[]{:S(2)}, u32[]{:S(2)}) collective-permute-start(f32[1,32,1536]{2,1,0:T(8,128)S(1)} %get-tuple-element.24), channel_id=1, source_target_pairs={{8,0},{16,8},{24,16},{32,24},{40,32},{48,40},{56,48},{64,56},{72,6... | collective-permute-start | bytes 589832 | tf_op jit(solution)/shard_map/ppermute | solution.py:15
  73.1 6.6 %collective-permute-start.5 = (f32[1,32,1536]{2,1,0:T(8,128)S(1)}, f32[1,32,1536]{2,1,0:T(8,128)S(1)}, u32[]{:S(2)}, u32[]{:S(2)}) collective-permute-start(f32[1,32,1536]{2,1,0:T(8,128)S(1)} %get-tuple-element.23), channel_id=1, source_target_pairs={{0,8},{8,16},{16,24},{24,32},{32,40},{40,48},{48,56},{56,64},{64,7... | collective-permute-start | bytes 589832 | tf_op jit(solution)/shard_map/ppermute | solution.py:12
  80.6 57.7 %collective-permute-start.6 = (f32[18,1,1536]{2,0,1:T(8,128)}, f32[18,1,1536]{2,0,1:T(8,128)}, u32[]{:S(2)}, u32[]{:S(2)}) collective-permute-start(f32[18,1,1536]{2,0,1:T(8,128)} %copy.42), channel_id=1, source_target_pairs={{1,0},{2,1},{3,2},{4,3},{5,4},{6,5},{7,6},{9,8},{10,9},{11,10},{12... | collective-permute-start | bytes 331784 | tf_op jit(solution)/shard_map/ppermute | solution.py:15
  83.1 56.1 %collective-permute-start.7 = (f32[18,1,1536]{2,0,1:T(8,128)}, f32[18,1,1536]{2,0,1:T(8,128)}, u32[]{:S(2)}, u32[]{:S(2)}) collective-permute-start(f32[18,1,1536]{2,0,1:T(8,128)} %copy.44), channel_id=1, source_target_pairs={{0,1},{1,2},{2,3},{3,4},{4,5},{5,6},{6,7},{8,9},{9,10},{10,11},{11... | collective-permute-start | bytes 331784 | tf_op jit(solution)/shard_map/ppermute | solution.py:12
  139.3 5.9 %slice-start = ((s8[4423680]{0:T(1024)(128)(4,1)}), s8[4194304]{0:T(1024)(128)(4,1)S(1)}, s32[]{:S(2)}) async-start(s8[4423680]{0:T(1024)(128)(4,1)} %bitcast.32), calls=%async_computation.2 | async-start | bytes 8388608
  140.5 4.7 %slice-start.1 = ((s8[4423680]{0:T(1024)(128)(4,1)}), s8[229376]{0:T(1024)(128)(4,1)S(1)}, s32[]{:S(2)}) async-start(s8[4423680]{0:T(1024)(128)(4,1)} %bitcast.32), calls=%async_computation.3 | async-start | bytes 458752
  202.0 13.7 %copy-start.3 = (f32[8,1,8,1,128,1]{4,2,0,5,3,1:T(8,128)S(1)}, f32[8,1,8,1,128,1]{4,2,0,5,3,1:T(8,128)}, u32[]{:S(2)}) copy-start(f32[8,1,8,1,128,1]{4,2,0,5,3,1:T(8,128)} %copy.64) | copy-start | bytes 98308
  223.4 148.1 %all-reduce.8.cloned.1.call-start = ((), (), s32[]{:S(2)}) async-start(), calls=%async_computation.1 | async-start | bytes 131072 | tf_op jit(solution)/shard_map/psum | solution.py:56
Sparse Core Ops, SparseCore 0:
  223.5 86.6 all-reduce.5
  312.5 58.8 all-reduce.7
